TPU v7x, 32 devices: a whole 2x2x4 slice. The times are simulated.
32 devices in a mesh: lev: 8 (over z, x), tile: 4 (over y, core).
Axes of the slice: x: 2, y: 2, z: 4, core: 2. Of those that a mesh axis runs over, the one named last changes fastest.
Arguments:
- increment: float32 [144, 96, 1440], P('lev', 'tile'), may hold values from -6 to 6
- kappa: float32 [144], P('lev'), may hold values from 0.02 to 0.24
- balance: float32 [144, 144], replicated, may hold values from -0.5 to 0.5
- correlation: float32 [144, 144], replicated, may hold values from -0.5 to 0.5
- ground_level: int32 [96, 1440], P('tile'), may hold values from 72 to 144
Outputs:
- covaried: float32 [144, 96, 1440], P('lev', 'tile')
Inputs may be any that keep to these rules, and one draw needn't show every extreme that they name: Levels from ground_level of a column down to the last one lie below ground.
All inputs are finite; a program needn't handle non-finite values.
Results may differ from a plain program's by a relative error of at most 0.00019.
Values sent between devices are 32-bit elements; how exact they have to be, the bound alone decides.
No kernel may reach another device: no remote copies, remote signals or barrier semaphores. Data moves between devices by JAX's collectives and lax.ppermute only.
A program may use at most 64 MiB of HBM per device.

v0:
```python
import jax
import jax.numpy as jnp
from jax import lax
from jax.sharding import PartitionSpec as P

PASSES = 10


def padded_2(value, sides, width):
    for axis, dim in sides:
        size, length = (lax.axis_size(axis), value.shape[dim])
        up = [(i, (i + 1) % size) for i in range(size - 1)]
        down = [(j, i) for i, j in up]
        last = lax.slice_in_dim(value, length - width, length, axis=dim)
        leading = lax.slice_in_dim(value, 0, width, axis=dim)
        before = lax.ppermute(last, axis, up)
        after = lax.ppermute(leading, axis, down)
        value = jnp.concatenate([before, value, after], axis=dim)
    return value


def local(increment, kappa, balance, correlation, ground_level):
    levels_here, lat_rows, lon_cells = increment.shape
    diffusivity = kappa[:, None, None]
    tile_start = lax.axis_index("tile") * lat_rows
    lat_total = lat_rows * lax.axis_size("tile")

    def sweep(padded, first_row):
        middle_rows = padded[:, 1:-1]
        beside = (
            padded[:, 2:]
            + padded[:, :-2]
            + jnp.roll(middle_rows, 1, 2)
            + jnp.roll(middle_rows, -1, 2)
        )
        result = middle_rows + diffusivity * (beside - 4.0 * middle_rows)
        global_rows = first_row + 1 + lax.broadcasted_iota(jnp.int32, (1, result.shape[1], 1), 1)
        inside = (global_rows >= 0) & (global_rows < lat_total)
        return jnp.where(inside, result, jnp.zeros((), jnp.float32))

    def two_passes(counter, state_field):
        padded = padded_2(state_field, (("tile", 1),), 2)
        return sweep(sweep(padded, tile_start - 2), tile_start - 1)

    smoothed = lax.fori_loop(0, PASSES // 2, two_passes, increment)
    flattened = smoothed.reshape(levels_here, lat_rows * lon_cells)
    group_size = lax.axis_size("lev")
    block_cols = lat_rows * lon_cells // group_size
    col_start = lax.axis_index("lev") * block_cols
    ground = lax.dynamic_slice_in_dim(
        ground_level.reshape(lat_rows * lon_cells), col_start, block_cols
    )
    total_levels = balance.shape[0]
    columns = lax.all_to_all(flattened, "lev", split_axis=1, concat_axis=0, tiled=True)
    mixed_cols = jnp.dot(
        balance, columns, precision=lax.Precision.HIGHEST, preferred_element_type=jnp.float32
    )
    mixed_cols = jnp.dot(
        correlation, mixed_cols, precision=lax.Precision.HIGHEST, preferred_element_type=jnp.float32
    )
    level_index = lax.broadcasted_iota(jnp.int32, (total_levels, 1), 0)
    mixed_cols = jnp.where(level_index < ground[None, :], mixed_cols, jnp.zeros((), jnp.float32))
    restored = lax.all_to_all(mixed_cols, "lev", split_axis=0, concat_axis=1, tiled=True)
    return restored.reshape(levels_here, lat_rows, lon_cells)


def solution(mesh):
    return jax.shard_map(
        local,
        mesh=mesh,
        in_specs=(P("lev", "tile", None), P("lev"), P(), P(), P("tile", None)),
        out_specs=P("lev", "tile", None),
        check_vma=False,
    )
```

profile of v0, /device:TPU:0, one launch (start us, length us, event | category | flops | bytes accessed | tf_op | source)
XLA Modules:
  0.0 272.3 jit_solution(930868567146244389)
XLA Ops:
  1.8 89.0 %while.12 = (s32[]{:T(128)}, f32[18,24,1440]{2,1,0:T(8,128)S(1)}, s32[]{:T(128)}, s32[]{:T(128)}, f32[18,1,1]{0,2,1:T(1,128)S(1)}, /*index=5*/s32[]{:T(128)}) while((s32[]{:T(128)}, f32[18,24,1440]{2,1,0:T(8,128)S(1)}, s32[]{:T(128)}, s32[]{:T(128)}, f32[18,1,1]{0,2,1:T(1,128)S(1)}, /*index=5*/s32[]{:T(128)}) %tuple.41), condition=%wide.region_1.2_spmd, body=%wide.region_0.1_spmd.sunk | while | flops 18455240 | bytes 57635248 | solution.py:45
  3.9 3.0 %collective-permute-start.1 = (f32[18,2,1440]{2,1,0:T(2,128)S(1)}, f32[18,2,1440]{2,1,0:T(2,128)S(1)}, u32[]{:S(2)}, u32[]{:S(2)}) collective-permute-start(f32[18,2,1440]{2,1,0:T(2,128)S(1)} %get-tuple-element.123), channel_id=1, source_target_pairs={{0,1},{1,2},{2,3},{4,5},{5,6},{6,7},{8,9},{9,10},{10,11},{12,13},{... | collective-permute-start | bytes 622088 | tf_op jit(solution)/shard_map/while/body/eval_jaxpr/ppermute | solution.py:16
  8.6 1.8 fusion.31
  10.4 3.1 %fusion.32 = f32[18,26,1440]{2,1,0:T(8,128)S(1)} fusion(f32[18,2,1440]{2,1,0:T(2,128)S(1)} %collective-permute-done, f32[18,24,1440]{2,1,0:T(8,128)S(1)} %get-tuple-element.137, f32[18,2,1440]{2,1,0:T(2,128)S(1)} %collective-permute-done.1, f32[18,26,1439]{2,1,0:T(8,128)S(1)} %get-tuple-element.124, f32[18,26,1439]{2,1,0:T(8,128)S(1)} %get-tuple-element.125, ...), kind=kLoop, calls=%fused_computation.6.clone.1 | loop fusion | flops 10782720 | bytes 13682114 | tf_op jit(solution)/shard_map/while/body/eval_jaxpr/jit(_where)/select_n | solution.py:39
  18.7 6.9 %collective-permute-start.1 = (f32[18,2,1440]{2,1,0:T(2,128)S(1)}, f32[18,2,1440]{2,1,0:T(2,128)S(1)}, u32[]{:S(2)}, u32[]{:S(2)}) collective-permute-start(f32[18,2,1440]{2,1,0:T(2,128)S(1)} %get-tuple-element.123), channel_id=1, source_target_pairs={{0,1},{1,2},{2,3},{4,5},{5,6},{6,7},{8,9},{9,10},{10,11},{12,13},{... | collective-permute-start | bytes 622088 | tf_op jit(solution)/shard_map/while/body/eval_jaxpr/ppermute | solution.py:16
  27.3 1.8 fusion.31
  29.1 3.1 %fusion.32 = f32[18,26,1440]{2,1,0:T(8,128)S(1)} fusion(f32[18,2,1440]{2,1,0:T(2,128)S(1)} %collective-permute-done, f32[18,24,1440]{2,1,0:T(8,128)S(1)} %get-tuple-element.137, f32[18,2,1440]{2,1,0:T(2,128)S(1)} %collective-permute-done.1, f32[18,26,1439]{2,1,0:T(8,128)S(1)} %get-tuple-element.124, f32[18,26,1439]{2,1,0:T(8,128)S(1)} %get-tuple-element.125, ...), kind=kLoop, calls=%fused_computation.6.clone.1 | loop fusion | flops 10782720 | bytes 13682114 | tf_op jit(solution)/shard_map/while/body/eval_jaxpr/jit(_where)/select_n | solution.py:39
  37.3 6.8 %collective-permute-start.1 = (f32[18,2,1440]{2,1,0:T(2,128)S(1)}, f32[18,2,1440]{2,1,0:T(2,128)S(1)}, u32[]{:S(2)}, u32[]{:S(2)}) collective-permute-start(f32[18,2,1440]{2,1,0:T(2,128)S(1)} %get-tuple-element.123), channel_id=1, source_target_pairs={{0,1},{1,2},{2,3},{4,5},{5,6},{6,7},{8,9},{9,10},{10,11},{12,13},{... | collective-permute-start | bytes 622088 | tf_op jit(solution)/shard_map/while/body/eval_jaxpr/ppermute | solution.py:16
  45.8 1.8 fusion.31
  47.6 3.1 %fusion.32 = f32[18,26,1440]{2,1,0:T(8,128)S(1)} fusion(f32[18,2,1440]{2,1,0:T(2,128)S(1)} %collective-permute-done, f32[18,24,1440]{2,1,0:T(8,128)S(1)} %get-tuple-element.137, f32[18,2,1440]{2,1,0:T(2,128)S(1)} %collective-permute-done.1, f32[18,26,1439]{2,1,0:T(8,128)S(1)} %get-tuple-element.124, f32[18,26,1439]{2,1,0:T(8,128)S(1)} %get-tuple-element.125, ...), kind=kLoop, calls=%fused_computation.6.clone.1 | loop fusion | flops 10782720 | bytes 13682114 | tf_op jit(solution)/shard_map/while/body/eval_jaxpr/jit(_where)/select_n | solution.py:39
  55.9 6.8 %collective-permute-start.1 = (f32[18,2,1440]{2,1,0:T(2,128)S(1)}, f32[18,2,1440]{2,1,0:T(2,128)S(1)}, u32[]{:S(2)}, u32[]{:S(2)}) collective-permute-start(f32[18,2,1440]{2,1,0:T(2,128)S(1)} %get-tuple-element.123), channel_id=1, source_target_pairs={{0,1},{1,2},{2,3},{4,5},{5,6},{6,7},{8,9},{9,10},{10,11},{12,13},{... | collective-permute-start | bytes 622088 | tf_op jit(solution)/shard_map/while/body/eval_jaxpr/ppermute | solution.py:16
  64.3 1.8 fusion.31
  66.1 3.1 %fusion.32 = f32[18,26,1440]{2,1,0:T(8,128)S(1)} fusion(f32[18,2,1440]{2,1,0:T(2,128)S(1)} %collective-permute-done, f32[18,24,1440]{2,1,0:T(8,128)S(1)} %get-tuple-element.137, f32[18,2,1440]{2,1,0:T(2,128)S(1)} %collective-permute-done.1, f32[18,26,1439]{2,1,0:T(8,128)S(1)} %get-tuple-element.124, f32[18,26,1439]{2,1,0:T(8,128)S(1)} %get-tuple-element.125, ...), kind=kLoop, calls=%fused_computation.6.clone.1 | loop fusion | flops 10782720 | bytes 13682114 | tf_op jit(solution)/shard_map/while/body/eval_jaxpr/jit(_where)/select_n | solution.py:39
  74.4 6.8 %collective-permute-start.1 = (f32[18,2,1440]{2,1,0:T(2,128)S(1)}, f32[18,2,1440]{2,1,0:T(2,128)S(1)}, u32[]{:S(2)}, u32[]{:S(2)}) collective-permute-start(f32[18,2,1440]{2,1,0:T(2,128)S(1)} %get-tuple-element.123), channel_id=1, source_target_pairs={{0,1},{1,2},{2,3},{4,5},{5,6},{6,7},{8,9},{9,10},{10,11},{12,13},{... | collective-permute-start | bytes 622088 | tf_op jit(solution)/shard_map/while/body/eval_jaxpr/ppermute | solution.py:16
  84.6 3.1 %fusion.32 = f32[18,26,1440]{2,1,0:T(8,128)S(1)} fusion(f32[18,2,1440]{2,1,0:T(2,128)S(1)} %collective-permute-done, f32[18,24,1440]{2,1,0:T(8,128)S(1)} %get-tuple-element.137, f32[18,2,1440]{2,1,0:T(2,128)S(1)} %collective-permute-done.1, f32[18,26,1439]{2,1,0:T(8,128)S(1)} %get-tuple-element.124, f32[18,26,1439]{2,1,0:T(8,128)S(1)} %get-tuple-element.125, ...), kind=kLoop, calls=%fused_computation.6.clone.1 | loop fusion | flops 10782720 | bytes 13682114 | tf_op jit(solution)/shard_map/while/body/eval_jaxpr/jit(_where)/select_n | solution.py:39
  90.8 1.9 all_to_all.26
  92.7 4.2 %copy.8 = f32[18,8,4320]{2,0,1:T(8,128)} copy(f32[18,8,4320]{2,1,0:T(8,128)} %all_to_all.26) | data formatting | bytes 4976640 | tf_op jit(solution)/shard_map/all_to_all | solution.py:54
  96.9 5.8 %all-to-all-start = ((f32[18,8,4320]{2,0,1:T(8,128)}), f32[18,8,4320]{2,0,1:T(8,128)S(1)}, u32[]{:S(2)}, u32[]{:S(2)}) async-start(f32[18,8,4320]{2,0,1:T(8,128)} %copy.8), calls=%async_computation | async-start | bytes 6684672 | tf_op jit(solution)/shard_map/all_to_all | solution.py:54
  105.2 71.3 %all-to-all-done = f32[18,8,4320]{2,0,1:T(8,128)S(1)} async-done(((f32[18,8,4320]{2,0,1:T(8,128)}), f32[18,8,4320]{2,0,1:T(8,128)S(1)}, u32[]{:S(2)}, u32[]{:S(2)}) %all-to-all-start) | async-done | bytes 2488352 | tf_op jit(solution)/shard_map/all_to_all | solution.py:54
  178.1 4.2 %fusion.19 = f32[4320,144]{0,1:T(8,128)S(1)} fusion(f32[144,4320]{1,0:T(8,128)} %all_to_all.29, f32[144,144]{1,0:T(8,128)S(1)} %copy-done), kind=kOutput, calls=%fused_computation.30 | convolution fusion | flops 1074954240 | bytes 5059584 | tf_op jit(solution)/shard_map/dot_general | solution.py:55
  182.3 3.9 %fusion.14 = f32[144,4320]{1,0:T(8,128)} fusion(f32[4320,144]{0,1:T(8,128)S(1)} %fusion.19, f32[144,144]{1,0:T(8,128)S(1)} %copy-done.2, s32[4320]{0:T(1024)S(1)} %dynamic_slice.3), kind=kOutput, calls=%fused_computation.24 | convolution fusion | flops 1076198400 | bytes 5076864 | tf_op jit(solution)/shard_map/dot_general | solution.py:58
  186.2 1.9 all_to_all.30
  188.1 81.2 %all_to_all.35 = f32[8,18,4320]{2,1,0:T(8,128)S(1)} all-to-all(f32[8,18,4320]{2,1,0:T(8,128)S(1)} %all_to_all.30), channel_id=1, replica_groups=mesh['lev'=8,'tile'=4] {'lev'}, dimensions={0} | all-to-all | bytes 4976640 | tf_op jit(solution)/shard_map/all_to_all | solution.py:63
  270.1 2.3 reshape.39
  (63 shorter events, 42.3 us)
Async XLA Ops:
  0.0 178.1 %copy-start = (f32[144,144]{1,0:T(8,128)S(1)}, f32[144,144]{1,0:T(8,128)}, u32[]{:S(2)}) copy-start(f32[144,144]{1,0:T(8,128)} %param.9) | copy-start | bytes 248836
  0.0 1.8 copy-start.1
  0.0 1.8 copy-start.3
  2.6 4.4 %collective-permute-start = (f32[18,2,1440]{2,1,0:T(2,128)}, f32[18,2,1440]{2,1,0:T(2,128)S(1)}, u32[]{:S(2)}, u32[]{:S(2)}) collective-permute-start(f32[18,2,1440]{2,1,0:T(2,128)} %get-tuple-element.122), channel_id=1, source_target_pairs={{1,0},{2,1},{3,2},{5,4},{6,5},{7,6},{9,8},{10,9},{11,10},{13,12},{... | collective-permute-start | bytes 622088 | tf_op jit(solution)/shard_map/while/body/eval_jaxpr/ppermute | solution.py:17
  3.9 4.1 %collective-permute-start.1 = (f32[18,2,1440]{2,1,0:T(2,128)S(1)}, f32[18,2,1440]{2,1,0:T(2,128)S(1)}, u32[]{:S(2)}, u32[]{:S(2)}) collective-permute-start(f32[18,2,1440]{2,1,0:T(2,128)S(1)} %get-tuple-element.123), channel_id=1, source_target_pairs={{0,1},{1,2},{2,3},{4,5},{5,6},{6,7},{8,9},{9,10},{10,11},{12,13},{... | collective-permute-start | bytes 622088 | tf_op jit(solution)/shard_map/while/body/eval_jaxpr/ppermute | solution.py:16
  17.4 8.3 %collective-permute-start = (f32[18,2,1440]{2,1,0:T(2,128)}, f32[18,2,1440]{2,1,0:T(2,128)S(1)}, u32[]{:S(2)}, u32[]{:S(2)}) collective-permute-start(f32[18,2,1440]{2,1,0:T(2,128)} %get-tuple-element.122), channel_id=1, source_target_pairs={{1,0},{2,1},{3,2},{5,4},{6,5},{7,6},{9,8},{10,9},{11,10},{13,12},{... | collective-permute-start | bytes 622088 | tf_op jit(solution)/shard_map/while/body/eval_jaxpr/ppermute | solution.py:17
  18.7 8.0 %collective-permute-start.1 = (f32[18,2,1440]{2,1,0:T(2,128)S(1)}, f32[18,2,1440]{2,1,0:T(2,128)S(1)}, u32[]{:S(2)}, u32[]{:S(2)}) collective-permute-start(f32[18,2,1440]{2,1,0:T(2,128)S(1)} %get-tuple-element.123), channel_id=1, source_target_pairs={{0,1},{1,2},{2,3},{4,5},{5,6},{6,7},{8,9},{9,10},{10,11},{12,13},{... | collective-permute-start | bytes 622088 | tf_op jit(solution)/shard_map/while/body/eval_jaxpr/ppermute | solution.py:16
  36.1 8.1 %collective-permute-start = (f32[18,2,1440]{2,1,0:T(2,128)}, f32[18,2,1440]{2,1,0:T(2,128)S(1)}, u32[]{:S(2)}, u32[]{:S(2)}) collective-permute-start(f32[18,2,1440]{2,1,0:T(2,128)} %get-tuple-element.122), channel_id=1, source_target_pairs={{1,0},{2,1},{3,2},{5,4},{6,5},{7,6},{9,8},{10,9},{11,10},{13,12},{... | collective-permute-start | bytes 622088 | tf_op jit(solution)/shard_map/while/body/eval_jaxpr/ppermute | solution.py:17
  37.3 7.9 %collective-permute-start.1 = (f32[18,2,1440]{2,1,0:T(2,128)S(1)}, f32[18,2,1440]{2,1,0:T(2,128)S(1)}, u32[]{:S(2)}, u32[]{:S(2)}) collective-permute-start(f32[18,2,1440]{2,1,0:T(2,128)S(1)} %get-tuple-element.123), channel_id=1, source_target_pairs={{0,1},{1,2},{2,3},{4,5},{5,6},{6,7},{8,9},{9,10},{10,11},{12,13},{... | collective-permute-start | bytes 622088 | tf_op jit(solution)/shard_map/while/body/eval_jaxpr/ppermute | solution.py:16
  54.6 8.1 %collective-permute-start = (f32[18,2,1440]{2,1,0:T(2,128)}, f32[18,2,1440]{2,1,0:T(2,128)S(1)}, u32[]{:S(2)}, u32[]{:S(2)}) collective-permute-start(f32[18,2,1440]{2,1,0:T(2,128)} %get-tuple-element.122), channel_id=1, source_target_pairs={{1,0},{2,1},{3,2},{5,4},{6,5},{7,6},{9,8},{10,9},{11,10},{13,12},{... | collective-permute-start | bytes 622088 | tf_op jit(solution)/shard_map/while/body/eval_jaxpr/ppermute | solution.py:17
  55.9 7.9 %collective-permute-start.1 = (f32[18,2,1440]{2,1,0:T(2,128)S(1)}, f32[18,2,1440]{2,1,0:T(2,128)S(1)}, u32[]{:S(2)}, u32[]{:S(2)}) collective-permute-start(f32[18,2,1440]{2,1,0:T(2,128)S(1)} %get-tuple-element.123), channel_id=1, source_target_pairs={{0,1},{1,2},{2,3},{4,5},{5,6},{6,7},{8,9},{9,10},{10,11},{12,13},{... | collective-permute-start | bytes 622088 | tf_op jit(solution)/shard_map/while/body/eval_jaxpr/ppermute | solution.py:16
  73.1 8.1 %collective-permute-start = (f32[18,2,1440]{2,1,0:T(2,128)}, f32[18,2,1440]{2,1,0:T(2,128)S(1)}, u32[]{:S(2)}, u32[]{:S(2)}) collective-permute-start(f32[18,2,1440]{2,1,0:T(2,128)} %get-tuple-element.122), channel_id=1, source_target_pairs={{1,0},{2,1},{3,2},{5,4},{6,5},{7,6},{9,8},{10,9},{11,10},{13,12},{... | collective-permute-start | bytes 622088 | tf_op jit(solution)/shard_map/while/body/eval_jaxpr/ppermute | solution.py:17
  74.4 7.9 %collective-permute-start.1 = (f32[18,2,1440]{2,1,0:T(2,128)S(1)}, f32[18,2,1440]{2,1,0:T(2,128)S(1)}, u32[]{:S(2)}, u32[]{:S(2)}) collective-permute-start(f32[18,2,1440]{2,1,0:T(2,128)S(1)} %get-tuple-element.123), channel_id=1, source_target_pairs={{0,1},{1,2},{2,3},{4,5},{5,6},{6,7},{8,9},{9,10},{10,11},{12,13},{... | collective-permute-start | bytes 622088 | tf_op jit(solution)/shard_map/while/body/eval_jaxpr/ppermute | solution.py:16
  96.9 79.6 %all-to-all-start = ((f32[18,8,4320]{2,0,1:T(8,128)}), f32[18,8,4320]{2,0,1:T(8,128)S(1)}, u32[]{:S(2)}, u32[]{:S(2)}) async-start(f32[18,8,4320]{2,0,1:T(8,128)} %copy.8), calls=%async_computation | async-start | bytes 6684672 | tf_op jit(solution)/shard_map/all_to_all | solution.py:54
  178.1 4.2 %copy-start.2 = (f32[144,144]{1,0:T(8,128)S(1)}, f32[144,144]{1,0:T(8,128)}, u32[]{:S(2)}) copy-start(f32[144,144]{1,0:T(8,128)} %param.10) | copy-start | bytes 248836
where the time goes:
time: 273 us; the launch traced here: 272 us
  blocking collectives  81.2 us (30%)
  waiting for transfers between devices  76.4 us (28%)
  starting transfers between devices  42.6 us (16%)
  local copies, waits for them, and re-layouts  37 us (14%)
  other arithmetic  26.6 us (10%)
  matrix products  8.1 us (3%)
    all_to_all x1, blocking collectives, local(): lax.all_to_all(mixed_cols, 'lev', split_axis=0, concat_axis=1, tiled=True)  81.2 us
    all_to_all x1, waiting for transfers between devices, local(): lax.all_to_all(flattened, 'lev', split_axis=1, concat_axis=0, tiled=True)  71.3 us
    ppermute x5, starting transfers between devices, padded_2(): before = lax.ppermute(last, axis, up)  30.4 us
    select_n x10, other arithmetic, sweep(): return jnp.where(inside, result, jnp.zeros((), jnp.float32))  23.7 us
    slice x15, local copies, waits for them, and re-layouts, sweep(): jnp.roll(middle_rows, -1, 2)  15.8 us
    all_to_all x3, local copies, waits for them, and re-layouts, local(): lax.all_to_all(flattened, 'lev', split_axis=1, concat_axis=0, tiled=True)  7.75 us
    ppermute x5, starting transfers between devices, padded_2(): after = lax.ppermute(leading, axis, down)  6.4 us
    all_to_all x1, starting transfers between devices, local(): lax.all_to_all(flattened, 'lev', split_axis=1, concat_axis=0, tiled=True)  5.81 us
  transfers between devices with their start and end apart: 11, of which 6 were waited for; matrix products, arithmetic and copies ran while one was open for 1% of the time, Pallas kernels for 0%

commit v1 on v0

--- a/solution.py
+++ b/solution.py
@@ -51,7 +51,10 @@
         ground_level.reshape(lat_rows * lon_cells), col_start, block_cols
     )
     total_levels = balance.shape[0]
-    columns = lax.all_to_all(flattened, "lev", split_axis=1, concat_axis=0, tiled=True)
+    count = lax.axis_size("lev")
+    shards = jnp.stack(jnp.split(flattened, count, axis=1), axis=0)
+    shards = lax.all_to_all(shards, "lev", split_axis=0, concat_axis=0)
+    columns = jnp.concatenate(shards, axis=0)
     mixed_cols = jnp.dot(
         balance, columns, precision=lax.Precision.HIGHEST, preferred_element_type=jnp.float32
     )

time: 273 us -> 282 us (1.033)
  local copies, waits for them, and re-layouts: 37 us -> 45.8 us
    unnamed x8 -> x17, local copies, waits for them, and re-layouts: 1.8 us -> 12.3 us
    all_to_all x3 -> x0, local copies, waits for them, and re-layouts: 7.75 us -> none  [local(): lax.all_to_all(flattened, 'lev', split_axis=1, concat_axis=0, tiled=True)]
    reshape x0 -> x2, local copies, waits for them, and re-layouts: none -> 5.18 us  [the longest x1 3.56 us: local(): flattened = smoothed.reshape(levels_here, lat_rows * lon_cells)]
where the time goes in v1:
time: 282 us; the launch traced here: 281 us
  blocking collectives  81.2 us (29%)
  waiting for transfers between devices  76.4 us (27%)
  local copies, waits for them, and re-layouts  45.8 us (16%)
  starting transfers between devices  42.6 us (15%)
  other arithmetic  26.6 us (9%)
  matrix products  8.1 us (3%)
    all_to_all x1, blocking collectives, local(): lax.all_to_all(mixed_cols, 'lev', split_axis=0, concat_axis=1, tiled=True)  81.2 us
    all_to_all x1, waiting for transfers between devices, local(): shards = lax.all_to_all(shards, 'lev', split_axis=0, concat_axis=0)  71.3 us
    ppermute x5, starting transfers between devices, padded_2(): before = lax.ppermute(last, axis, up)  30.4 us
    select_n x10, other arithmetic, sweep(): return jnp.where(inside, result, jnp.zeros((), jnp.float32))  23.7 us
    slice x15, local copies, waits for them, and re-layouts, sweep(): jnp.roll(middle_rows, -1, 2)  15.8 us
    unnamed x17, local copies, waits for them, and re-layouts  12.3 us
    ppermute x5, starting transfers between devices, padded_2(): after = lax.ppermute(leading, axis, down)  6.4 us
    all_to_all x1, starting transfers between devices, local(): shards = lax.all_to_all(shards, 'lev', split_axis=0, concat_axis=0)  5.81 us
  transfers between devices with their start and end apart: 11, of which 6 were waited for; matrix products, arithmetic and copies ran while one was open for 1% of the time, Pallas kernels for 0%

profile of v1, /device:TPU:0, one launch (start us, length us, event | category | flops | bytes accessed | tf_op | source)
XLA Modules:
  0.0 281.2 jit_solution(15106866871369911760)
XLA Ops:
  1.8 89.0 %while.12 = (s32[]{:T(128)}, f32[18,24,1440]{2,1,0:T(8,128)S(1)}, s32[]{:T(128)}, s32[]{:T(128)}, f32[18,1,1]{0,2,1:T(1,128)S(1)}, /*index=5*/s32[]{:T(128)}) while((s32[]{:T(128)}, f32[18,24,1440]{2,1,0:T(8,128)S(1)}, s32[]{:T(128)}, s32[]{:T(128)}, f32[18,1,1]{0,2,1:T(1,128)S(1)}, /*index=5*/s32[]{:T(128)}) %tuple.41), condition=%wide.region_1.2_spmd, body=%wide.region_0.1_spmd.sunk | while | flops 18455240 | bytes 57635248 | solution.py:45
  3.9 3.0 %collective-permute-start.1 = (f32[18,2,1440]{2,1,0:T(2,128)S(1)}, f32[18,2,1440]{2,1,0:T(2,128)S(1)}, u32[]{:S(2)}, u32[]{:S(2)}) collective-permute-start(f32[18,2,1440]{2,1,0:T(2,128)S(1)} %get-tuple-element.123), channel_id=1, source_target_pairs={{0,1},{1,2},{2,3},{4,5},{5,6},{6,7},{8,9},{9,10},{10,11},{12,13},{... | collective-permute-start | bytes 622088 | tf_op jit(solution)/shard_map/while/body/eval_jaxpr/ppermute | solution.py:16
  8.6 1.8 fusion.39
  10.4 3.1 %fusion.40 = f32[18,26,1440]{2,1,0:T(8,128)S(1)} fusion(f32[18,2,1440]{2,1,0:T(2,128)S(1)} %collective-permute-done, f32[18,24,1440]{2,1,0:T(8,128)S(1)} %get-tuple-element.137, f32[18,2,1440]{2,1,0:T(2,128)S(1)} %collective-permute-done.1, f32[18,26,1439]{2,1,0:T(8,128)S(1)} %get-tuple-element.124, f32[18,26,1439]{2,1,0:T(8,128)S(1)} %get-tuple-element.125, ...), kind=kLoop, calls=%fused_computation.6.clone.1 | loop fusion | flops 10782720 | bytes 13682114 | tf_op jit(solution)/shard_map/while/body/eval_jaxpr/jit(_where)/select_n | solution.py:39
  18.7 6.9 %collective-permute-start.1 = (f32[18,2,1440]{2,1,0:T(2,128)S(1)}, f32[18,2,1440]{2,1,0:T(2,128)S(1)}, u32[]{:S(2)}, u32[]{:S(2)}) collective-permute-start(f32[18,2,1440]{2,1,0:T(2,128)S(1)} %get-tuple-element.123), channel_id=1, source_target_pairs={{0,1},{1,2},{2,3},{4,5},{5,6},{6,7},{8,9},{9,10},{10,11},{12,13},{... | collective-permute-start | bytes 622088 | tf_op jit(solution)/shard_map/while/body/eval_jaxpr/ppermute | solution.py:16
  29.1 3.1 %fusion.40 = f32[18,26,1440]{2,1,0:T(8,128)S(1)} fusion(f32[18,2,1440]{2,1,0:T(2,128)S(1)} %collective-permute-done, f32[18,24,1440]{2,1,0:T(8,128)S(1)} %get-tuple-element.137, f32[18,2,1440]{2,1,0:T(2,128)S(1)} %collective-permute-done.1, f32[18,26,1439]{2,1,0:T(8,128)S(1)} %get-tuple-element.124, f32[18,26,1439]{2,1,0:T(8,128)S(1)} %get-tuple-element.125, ...), kind=kLoop, calls=%fused_computation.6.clone.1 | loop fusion | flops 10782720 | bytes 13682114 | tf_op jit(solution)/shard_map/while/body/eval_jaxpr/jit(_where)/select_n | solution.py:39
  37.3 6.8 %collective-permute-start.1 = (f32[18,2,1440]{2,1,0:T(2,128)S(1)}, f32[18,2,1440]{2,1,0:T(2,128)S(1)}, u32[]{:S(2)}, u32[]{:S(2)}) collective-permute-start(f32[18,2,1440]{2,1,0:T(2,128)S(1)} %get-tuple-element.123), channel_id=1, source_target_pairs={{0,1},{1,2},{2,3},{4,5},{5,6},{6,7},{8,9},{9,10},{10,11},{12,13},{... | collective-permute-start | bytes 622088 | tf_op jit(solution)/shard_map/while/body/eval_jaxpr/ppermute | solution.py:16
  47.6 3.1 %fusion.40 = f32[18,26,1440]{2,1,0:T(8,128)S(1)} fusion(f32[18,2,1440]{2,1,0:T(2,128)S(1)} %collective-permute-done, f32[18,24,1440]{2,1,0:T(8,128)S(1)} %get-tuple-element.137, f32[18,2,1440]{2,1,0:T(2,128)S(1)} %collective-permute-done.1, f32[18,26,1439]{2,1,0:T(8,128)S(1)} %get-tuple-element.124, f32[18,26,1439]{2,1,0:T(8,128)S(1)} %get-tuple-element.125, ...), kind=kLoop, calls=%fused_computation.6.clone.1 | loop fusion | flops 10782720 | bytes 13682114 | tf_op jit(solution)/shard_map/while/body/eval_jaxpr/jit(_where)/select_n | solution.py:39
  55.9 6.8 %collective-permute-start.1 = (f32[18,2,1440]{2,1,0:T(2,128)S(1)}, f32[18,2,1440]{2,1,0:T(2,128)S(1)}, u32[]{:S(2)}, u32[]{:S(2)}) collective-permute-start(f32[18,2,1440]{2,1,0:T(2,128)S(1)} %get-tuple-element.123), channel_id=1, source_target_pairs={{0,1},{1,2},{2,3},{4,5},{5,6},{6,7},{8,9},{9,10},{10,11},{12,13},{... | collective-permute-start | bytes 622088 | tf_op jit(solution)/shard_map/while/body/eval_jaxpr/ppermute | solution.py:16
  66.1 3.1 %fusion.40 = f32[18,26,1440]{2,1,0:T(8,128)S(1)} fusion(f32[18,2,1440]{2,1,0:T(2,128)S(1)} %collective-permute-done, f32[18,24,1440]{2,1,0:T(8,128)S(1)} %get-tuple-element.137, f32[18,2,1440]{2,1,0:T(2,128)S(1)} %collective-permute-done.1, f32[18,26,1439]{2,1,0:T(8,128)S(1)} %get-tuple-element.124, f32[18,26,1439]{2,1,0:T(8,128)S(1)} %get-tuple-element.125, ...), kind=kLoop, calls=%fused_computation.6.clone.1 | loop fusion | flops 10782720 | bytes 13682114 | tf_op jit(solution)/shard_map/while/body/eval_jaxpr/jit(_where)/select_n | solution.py:39
  74.4 6.8 %collective-permute-start.1 = (f32[18,2,1440]{2,1,0:T(2,128)S(1)}, f32[18,2,1440]{2,1,0:T(2,128)S(1)}, u32[]{:S(2)}, u32[]{:S(2)}) collective-permute-start(f32[18,2,1440]{2,1,0:T(2,128)S(1)} %get-tuple-element.123), channel_id=1, source_target_pairs={{0,1},{1,2},{2,3},{4,5},{5,6},{6,7},{8,9},{9,10},{10,11},{12,13},{... | collective-permute-start | bytes 622088 | tf_op jit(solution)/shard_map/while/body/eval_jaxpr/ppermute | solution.py:16
  84.6 3.1 %fusion.40 = f32[18,26,1440]{2,1,0:T(8,128)S(1)} fusion(f32[18,2,1440]{2,1,0:T(2,128)S(1)} %collective-permute-done, f32[18,24,1440]{2,1,0:T(8,128)S(1)} %get-tuple-element.137, f32[18,2,1440]{2,1,0:T(2,128)S(1)} %collective-permute-done.1, f32[18,26,1439]{2,1,0:T(8,128)S(1)} %get-tuple-element.124, f32[18,26,1439]{2,1,0:T(8,128)S(1)} %get-tuple-element.125, ...), kind=kLoop, calls=%fused_computation.6.clone.1 | loop fusion | flops 10782720 | bytes 13682114 | tf_op jit(solution)/shard_map/while/body/eval_jaxpr/jit(_where)/select_n | solution.py:39
  90.8 3.6 %reshape.40 = f32[18,34560]{1,0:T(8,128)} reshape(f32[18,24,1440]{2,1,0:T(8,128)S(1)} %get-tuple-element.64) | data formatting | bytes 4976640 | tf_op jit(solution)/shard_map/reshape | solution.py:46
  94.3 1.9 fusion.22
  96.3 1.9 fusion.21
  98.2 1.9 fusion.20
  100.2 1.9 fusion.19
  105.7 5.8 %all-to-all-start = ((f32[8,18,4320]{2,1,0:T(8,128)}), f32[8,18,4320]{2,1,0:T(8,128)S(1)}, u32[]{:S(2)}, u32[]{:S(2)}) async-start(f32[8,18,4320]{2,1,0:T(8,128)} %fusion.15), calls=%async_computation | async-start | bytes 6684672 | tf_op jit(solution)/shard_map/all_to_all | solution.py:56
  114.1 71.3 %all-to-all-done = f32[8,18,4320]{2,1,0:T(8,128)S(1)} async-done(((f32[8,18,4320]{2,1,0:T(8,128)}), f32[8,18,4320]{2,1,0:T(8,128)S(1)}, u32[]{:S(2)}, u32[]{:S(2)}) %all-to-all-start) | async-done | bytes 2488352 | tf_op jit(solution)/shard_map/all_to_all | solution.py:56
  186.9 4.2 %fusion.27 = f32[4320,144]{0,1:T(8,128)S(1)} fusion(f32[144,4320]{1,0:T(8,128)} %reshape.41, f32[144,144]{1,0:T(8,128)S(1)} %copy-done), kind=kOutput, calls=%fused_computation.46 | convolution fusion | flops 1074954240 | bytes 5059584 | tf_op jit(solution)/shard_map/dot_general | solution.py:58
  191.1 3.9 %fusion.14 = f32[144,4320]{1,0:T(8,128)} fusion(f32[4320,144]{0,1:T(8,128)S(1)} %fusion.27, f32[144,144]{1,0:T(8,128)S(1)} %copy-done.3, s32[4320]{0:T(1024)S(1)} %dynamic_slice.3), kind=kOutput, calls=%fused_computation.24 | convolution fusion | flops 1076198400 | bytes 5076864 | tf_op jit(solution)/shard_map/dot_general | solution.py:61
  195.1 1.9 all_to_all.16
  196.9 81.2 %all_to_all.21 = f32[8,18,4320]{2,1,0:T(8,128)S(1)} all-to-all(f32[8,18,4320]{2,1,0:T(8,128)S(1)} %all_to_all.16), channel_id=1, replica_groups=mesh['lev'=8,'tile'=4] {'lev'}, dimensions={0} | all-to-all | bytes 4976640 | tf_op jit(solution)/shard_map/all_to_all | solution.py:66
  278.9 2.3 reshape.42
  (72 shorter events, 51.3 us)
Async XLA Ops:
  0.0 186.9 %copy-start = (f32[144,144]{1,0:T(8,128)S(1)}, f32[144,144]{1,0:T(8,128)}, u32[]{:S(2)}) copy-start(f32[144,144]{1,0:T(8,128)} %param.9) | copy-start | bytes 248836
  0.0 1.8 copy-start.1
  0.0 1.8 copy-start.4
  2.6 4.4 %collective-permute-start = (f32[18,2,1440]{2,1,0:T(2,128)}, f32[18,2,1440]{2,1,0:T(2,128)S(1)}, u32[]{:S(2)}, u32[]{:S(2)}) collective-permute-start(f32[18,2,1440]{2,1,0:T(2,128)} %get-tuple-element.122), channel_id=1, source_target_pairs={{1,0},{2,1},{3,2},{5,4},{6,5},{7,6},{9,8},{10,9},{11,10},{13,12},{... | collective-permute-start | bytes 622088 | tf_op jit(solution)/shard_map/while/body/eval_jaxpr/ppermute | solution.py:17
  3.9 4.1 %collective-permute-start.1 = (f32[18,2,1440]{2,1,0:T(2,128)S(1)}, f32[18,2,1440]{2,1,0:T(2,128)S(1)}, u32[]{:S(2)}, u32[]{:S(2)}) collective-permute-start(f32[18,2,1440]{2,1,0:T(2,128)S(1)} %get-tuple-element.123), channel_id=1, source_target_pairs={{0,1},{1,2},{2,3},{4,5},{5,6},{6,7},{8,9},{9,10},{10,11},{12,13},{... | collective-permute-start | bytes 622088 | tf_op jit(solution)/shard_map/while/body/eval_jaxpr/ppermute | solution.py:16
  17.4 8.3 %collective-permute-start = (f32[18,2,1440]{2,1,0:T(2,128)}, f32[18,2,1440]{2,1,0:T(2,128)S(1)}, u32[]{:S(2)}, u32[]{:S(2)}) collective-permute-start(f32[18,2,1440]{2,1,0:T(2,128)} %get-tuple-element.122), channel_id=1, source_target_pairs={{1,0},{2,1},{3,2},{5,4},{6,5},{7,6},{9,8},{10,9},{11,10},{13,12},{... | collective-permute-start | bytes 622088 | tf_op jit(solution)/shard_map/while/body/eval_jaxpr/ppermute | solution.py:17
  18.7 8.0 %collective-permute-start.1 = (f32[18,2,1440]{2,1,0:T(2,128)S(1)}, f32[18,2,1440]{2,1,0:T(2,128)S(1)}, u32[]{:S(2)}, u32[]{:S(2)}) collective-permute-start(f32[18,2,1440]{2,1,0:T(2,128)S(1)} %get-tuple-element.123), channel_id=1, source_target_pairs={{0,1},{1,2},{2,3},{4,5},{5,6},{6,7},{8,9},{9,10},{10,11},{12,13},{... | collective-permute-start | bytes 622088 | tf_op jit(solution)/shard_map/while/body/eval_jaxpr/ppermute | solution.py:16
  36.1 8.1 %collective-permute-start = (f32[18,2,1440]{2,1,0:T(2,128)}, f32[18,2,1440]{2,1,0:T(2,128)S(1)}, u32[]{:S(2)}, u32[]{:S(2)}) collective-permute-start(f32[18,2,1440]{2,1,0:T(2,128)} %get-tuple-element.122), channel_id=1, source_target_pairs={{1,0},{2,1},{3,2},{5,4},{6,5},{7,6},{9,8},{10,9},{11,10},{13,12},{... | collective-permute-start | bytes 622088 | tf_op jit(solution)/shard_map/while/body/eval_jaxpr/ppermute | solution.py:17
  37.3 7.9 %collective-permute-start.1 = (f32[18,2,1440]{2,1,0:T(2,128)S(1)}, f32[18,2,1440]{2,1,0:T(2,128)S(1)}, u32[]{:S(2)}, u32[]{:S(2)}) collective-permute-start(f32[18,2,1440]{2,1,0:T(2,128)S(1)} %get-tuple-element.123), channel_id=1, source_target_pairs={{0,1},{1,2},{2,3},{4,5},{5,6},{6,7},{8,9},{9,10},{10,11},{12,13},{... | collective-permute-start | bytes 622088 | tf_op jit(solution)/shard_map/while/body/eval_jaxpr/ppermute | solution.py:16
  54.6 8.1 %collective-permute-start = (f32[18,2,1440]{2,1,0:T(2,128)}, f32[18,2,1440]{2,1,0:T(2,128)S(1)}, u32[]{:S(2)}, u32[]{:S(2)}) collective-permute-start(f32[18,2,1440]{2,1,0:T(2,128)} %get-tuple-element.122), channel_id=1, source_target_pairs={{1,0},{2,1},{3,2},{5,4},{6,5},{7,6},{9,8},{10,9},{11,10},{13,12},{... | collective-permute-start | bytes 622088 | tf_op jit(solution)/shard_map/while/body/eval_jaxpr/ppermute | solution.py:17
  55.9 7.9 %collective-permute-start.1 = (f32[18,2,1440]{2,1,0:T(2,128)S(1)}, f32[18,2,1440]{2,1,0:T(2,128)S(1)}, u32[]{:S(2)}, u32[]{:S(2)}) collective-permute-start(f32[18,2,1440]{2,1,0:T(2,128)S(1)} %get-tuple-element.123), channel_id=1, source_target_pairs={{0,1},{1,2},{2,3},{4,5},{5,6},{6,7},{8,9},{9,10},{10,11},{12,13},{... | collective-permute-start | bytes 622088 | tf_op jit(solution)/shard_map/while/body/eval_jaxpr/ppermute | solution.py:16
  73.1 8.1 %collective-permute-start = (f32[18,2,1440]{2,1,0:T(2,128)}, f32[18,2,1440]{2,1,0:T(2,128)S(1)}, u32[]{:S(2)}, u32[]{:S(2)}) collective-permute-start(f32[18,2,1440]{2,1,0:T(2,128)} %get-tuple-element.122), channel_id=1, source_target_pairs={{1,0},{2,1},{3,2},{5,4},{6,5},{7,6},{9,8},{10,9},{11,10},{13,12},{... | collective-permute-start | bytes 622088 | tf_op jit(solution)/shard_map/while/body/eval_jaxpr/ppermute | solution.py:17
  74.4 7.9 %collective-permute-start.1 = (f32[18,2,1440]{2,1,0:T(2,128)S(1)}, f32[18,2,1440]{2,1,0:T(2,128)S(1)}, u32[]{:S(2)}, u32[]{:S(2)}) collective-permute-start(f32[18,2,1440]{2,1,0:T(2,128)S(1)} %get-tuple-element.123), channel_id=1, source_target_pairs={{0,1},{1,2},{2,3},{4,5},{5,6},{6,7},{8,9},{9,10},{10,11},{12,13},{... | collective-permute-start | bytes 622088 | tf_op jit(solution)/shard_map/while/body/eval_jaxpr/ppermute | solution.py:16
  94.3 7.8 %copy-start.2 = (f32[18,34560]{1,0:T(8,128)S(1)}, f32[18,34560]{1,0:T(8,128)}, u32[]{:S(2)}) copy-start(f32[18,34560]{1,0:T(8,128)} %reshape.40) | copy-start | bytes 7464964
  105.7 79.6 %all-to-all-start = ((f32[8,18,4320]{2,1,0:T(8,128)}), f32[8,18,4320]{2,1,0:T(8,128)S(1)}, u32[]{:S(2)}, u32[]{:S(2)}) async-start(f32[8,18,4320]{2,1,0:T(8,128)} %fusion.15), calls=%async_computation | async-start | bytes 6684672 | tf_op jit(solution)/shard_map/all_to_all | solution.py:56
  186.9 4.2 %copy-start.3 = (f32[144,144]{1,0:T(8,128)S(1)}, f32[144,144]{1,0:T(8,128)}, u32[]{:S(2)}) copy-start(f32[144,144]{1,0:T(8,128)} %param.10) | copy-start | bytes 248836
